TPU v7x, 256 devices: a whole 4x4x8 slice. The times are simulated.
256 devices in a mesh: wide: 32 (over z, x_lo, core), tm: 8 (over x_hi, y).
Axes of the slice: x: 4 (x_hi: 2, x_lo: 2; x = x_hi * 2 + x_lo), y: 4, z: 8, core: 2. Of those that a mesh axis runs over, the one named last changes fastest.
Arguments:
- clips_in: bfloat16 [32, 32, 14, 14, 256], P('wide', 'tm'), may hold values from -6 to 6
- w_spatial: bfloat16 [3, 3, 256, 256], replicated, may hold values from -0.125 to 0.125
- w_temporal: bfloat16 [3, 256, 256], replicated, may hold values from -0.21875 to 0.21875
- w_proj: bfloat16 [256, 512], replicated, may hold values from -0.375 to 0.375
- prompts: bfloat16 [4096, 512], P('tm'), may hold values from -6 to 6
- positives: int32 [32, 4], P('wide'), may hold values from 0 to 4095
Outputs:
- grad_spatial: float32 [3, 3, 256, 256], replicated
- grad_temporal: float32 [3, 256, 256], replicated
- grad_proj: float32 [256, 512], replicated
- grad_prompts: float32 [4096, 512], P('tm')
Inputs may be any that keep to these rules, and one draw needn't show every extreme that they name: `positives`: 4 positive prompt ids for each clip; a clip may name one id more than once.
All inputs are finite; a program needn't handle non-finite values.
Results may differ from a plain program's by a relative error of at most 0.0037.
Values may be sent and summed in bfloat16 or wider, within the bound.
A program may use at most 64 MiB of HBM per device.

v0:
```python
import jax
import jax.numpy as jnp
from jax import lax
from jax.sharding import PartitionSpec as P

HI = lax.Precision.HIGHEST


def extended(block, sides, width):
    for axis, dim in sides:
        count = lax.axis_size(axis)
        forward = [(i, i + 1) for i in range(count - 1)]
        backward = [(target, source) for source, target in forward]
        low = lax.ppermute(
            lax.slice_in_dim(block, block.shape[dim] - width, None, axis=dim), axis, forward
        )
        high = lax.ppermute(lax.slice_in_dim(block, 0, width, axis=dim), axis, backward)
        block = jnp.concatenate([low, block, high], axis=dim)
    return block


def dsilu(v):
    sig = jax.nn.sigmoid(v)
    return sig * (1.0 + v * (1.0 - sig))


def contract(left, right):
    return lax.dot_general(
        left, right, (((0,), (0,)), ((), ())), preferred_element_type=jnp.float32
    )


def count_hits(pos_ids, ids):
    return jnp.sum((pos_ids[:, :, None] == ids[None, None, :]).astype(jnp.float32), axis=1)


def body(clips_in, w_spatial, w_temporal, w_proj, prompts, positives):
    clips, frames, side, unused, chan = clips_in.shape
    rows = clips * frames * side * side
    padded = jnp.pad(clips_in, ((0, 0), (0, 0), (1, 1), (1, 1), (0, 0)))
    pre_s = jnp.zeros((rows, chan), jnp.float32)
    for a in range(3):
        for b in range(3):
            window = padded[:, :, a : a + side, b : b + side, :].reshape(rows, chan)
            pre_s = pre_s + jnp.dot(window, w_spatial[a, b], preferred_element_type=jnp.float32)
    act = jax.nn.silu(pre_s).astype(jnp.bfloat16).reshape(clips, frames, side, side, chan)
    act_wide = extended(act, (("tm", 1),), 1)
    pre_t = jnp.zeros((rows, chan), jnp.float32)
    for t in range(3):
        pre_t = pre_t + jnp.dot(
            act_wide[:, t : t + frames].reshape(rows, chan),
            w_temporal[t],
            preferred_element_type=jnp.float32,
        )
    out = clips_in.reshape(rows, chan).astype(jnp.float32) + jax.nn.silu(pre_t)
    pooled_loc = jnp.sum(out.reshape(clips, frames * side * side, chan), axis=1)
    pooled = lax.psum(pooled_loc, "tm")
    proj32 = w_proj.astype(jnp.float32)
    z = jnp.dot(pooled, proj32, precision=HI)
    znorm = jnp.sqrt(jnp.sum(z * z, axis=1, keepdims=True) + 1e-06)
    zhat = z / znorm
    p32 = prompts.astype(jnp.float32)
    pnorm = jnp.sqrt(jnp.sum(p32 * p32, axis=1, keepdims=True) + 1e-06)
    phat = p32 / pnorm
    expo = jnp.exp(16.0 * jnp.dot(zhat, phat.T, precision=HI))
    shard = phat.shape[0]
    ids = lax.axis_index("tm") * shard + jnp.arange(shard, dtype=jnp.int32)
    multi = count_hits(positives, ids)
    pos_expo = multi * expo
    total, pos_total = lax.psum(
        (jnp.sum(expo, axis=1, keepdims=True), jnp.sum(pos_expo, axis=1, keepdims=True)), "tm"
    )
    g_s = expo / total - pos_expo / pos_total
    g_zhat = lax.psum(16.0 * jnp.dot(g_s, phat, precision=HI), "tm")
    g_phat = lax.psum(16.0 * jnp.dot(g_s.T, zhat, precision=HI), "wide")
    grad_prompts = (g_phat - phat * jnp.sum(phat * g_phat, axis=1, keepdims=True)) / pnorm
    g_z = (g_zhat - zhat * jnp.sum(zhat * g_zhat, axis=1, keepdims=True)) / znorm
    proj_term = jnp.dot(pooled_loc.T, g_z, precision=HI)
    g_pooled = jnp.dot(g_z, proj32.T, precision=HI)
    g_t = (g_pooled[:, None, :] * dsilu(pre_t).reshape(clips, frames * side * side, chan)).astype(
        jnp.bfloat16
    )
    g_t_flat = g_t.reshape(rows, chan)
    temporal_term = jnp.stack(
        [contract(act_wide[:, t : t + frames].reshape(rows, chan), g_t_flat) for t in range(3)]
    )
    g_wide = extended(g_t.reshape(clips, frames, side, side, chan), (("tm", 1),), 1)
    g_act = jnp.zeros((rows, chan), jnp.float32)
    for t in range(3):
        g_act = g_act + jnp.dot(
            g_wide[:, 2 - t : 2 - t + frames].reshape(rows, chan),
            w_temporal[t].T,
            preferred_element_type=jnp.float32,
        )
    g_sp = (g_act * dsilu(pre_s)).astype(jnp.bfloat16)
    spatial_term = jnp.stack(
        [
            jnp.stack(
                [
                    contract(padded[:, :, a : a + side, b : b + side, :].reshape(rows, chan), g_sp)
                    for b in range(3)
                ]
            )
            for a in range(3)
        ]
    )
    spatial_sum, temporal_sum, proj_sum = lax.psum(
        (spatial_term, temporal_term, proj_term), ("wide", "tm")
    )
    return (spatial_sum, temporal_sum, proj_sum, grad_prompts)


def solution(mesh):
    placed = (P("wide", "tm", None, None, None), P(), P(), P(), P("tm", None), P("wide", None))
    return jax.shard_map(
        body, mesh=mesh, in_specs=placed, out_specs=(P(), P(), P(), P("tm", None)), check_vma=False
    )
```

profile of v0, /device:TPU:1, one launch (start us, length us, event | category | flops | bytes accessed | tf_op | source)
XLA Modules:
  0.0 645.0 jit_solution(18042460652931843559)
XLA Ops:
  7.2 1.1 copy.23
  8.3 3.9 pad_slice_fusion.1
  12.4 1.1 copy.29
  14.2 1.2 copy.27
  15.6 1.2 copy.28
  16.8 0.9 reshape.209
  17.6 1.1 copy.30
  18.7 0.9 reshape.211
  19.8 1.3 fusion.23
  22.7 0.7 copy-done.11
  23.9 0.7 copy-done.20
  24.7 1.2 multiply_convert_fusion.1
  26.0 4.0 collective-permute-start
  30.1 1.3 collective-permute-start.1
  31.6 2.1 fusion.11
  33.7 2.0 collective-permute-done.1
  35.7 1.0 pad_maximum_fusion.5
  36.7 0.9 reshape.213
  37.7 1.3 fusion.7
  39.0 2.2 add_reduce_fusion
  41.2 20.1 %psum.56 = f32[256]{0:T(256)S(1)} all-reduce(f32[256]{0:T(256)S(1)} %get-tuple-element.29), channel_id=1, replica_groups=mesh['wide'=32,'tm'=8] {'tm'}, use_global_device_ids=true, to_apply=%region_1.2 | all-reduce | flops 256 | bytes 2048 | tf_op jit(solution)/shard_map/psum | solution.py:57
  61.5 0.6 multiply_reduce_fusion.2
  62.9 1.0 fusion.46
  63.9 0.7 fusion.43
  64.6 16.2 %all-reduce.2 = (f32[]{:T(128)}, f32[]{:T(128)}) all-reduce(f32[]{:T(128)} %get-tuple-element.5, f32[]{:T(128)} %get-tuple-element.4), channel_id=1, replica_groups=mesh['wide'=32,'tm'=8] {'tm'}, use_global_device_ids=true, to_apply=%region_8.9 | all-reduce | flops 2 | bytes 16 | tf_op jit(solution)/shard_map/psum | solution.py:70
  80.8 1.3 divide_subtract_fusion
  82.2 0.7 fusion.45
  82.9 19.7 %psum.59 = f32[1,512]{1,0:T(1,128)S(1)} all-reduce(f32[1,512]{1,0:T(1,128)S(1)} %bitcast.147), channel_id=1, replica_groups=mesh['wide'=32,'tm'=8] {'tm'}, use_global_device_ids=true, to_apply=%region_9.10 | all-reduce | flops 512 | bytes 4096 | tf_op jit(solution)/shard_map/psum | solution.py:74
  102.6 0.6 multiply_reduce_fusion.1
  103.2 0.6 broadcast_multiply_fusion.1
  103.9 0.3 fusion.40
  104.2 1.4 multiply_convert_fusion
  105.6 1.1 convolution_bitcast_fusion
  106.7 1.1 convolution_bitcast_fusion.1
  107.7 0.3 convolution_bitcast_fusion.2
  108.2 2.1 fusion.9
  110.3 1.1 multiply_multiply_fusion
  111.5 1.4 collective-permute-start.2
  112.9 4.0 collective-permute-start.3
  116.9 0.9 broadcast_multiply_fusion
  118.1 0.9 pad_maximum_fusion.1
  119.1 0.9 reshape.218
  120.1 1.3 fusion.5
  121.6 1.5 fusion.3
  123.1 0.4 convolution_bitcast_fusion.3
  123.5 0.3 convolution_bitcast_fusion.4
  124.1 0.3 convolution_bitcast_fusion.5
  124.5 0.3 convolution_bitcast_fusion.6
  124.9 0.4 convolution_bitcast_fusion.7
  125.3 0.6 copy-done.8
  125.8 0.3 convolution_bitcast_fusion.8
  126.2 0.3 convolution_bitcast_fusion.9
  126.6 0.4 convolution_bitcast_fusion.10
  127.0 0.3 copy-done.14
  127.2 0.3 convolution_bitcast_fusion.11
  127.7 1.6 pad_maximum_fusion
  129.3 229.8 %all-reduce.6.cloned.1.call-done = f32[512,512]{1,0:T(8,128)} async-done(((f32[512,512]{1,0:T(8,128)}), f32[512,512]{1,0:T(8,128)}) %all-reduce.6.cloned.1.call-update) | async-done | bytes 1048592 | tf_op jit(solution)/shard_map/psum | solution.py:75
  359.1 1.6 multiply_reduce_fusion
  360.7 1.2 subtract_divide_fusion
  362.0 270.8 %all-reduce.8.cloned.1.call-done = (f32[3,3,256,256]{3,2,1,0:T(8,128)}, f32[3,256,256]{2,1,0:T(8,128)}, f32[256,512]{1,0:T(8,128)}) async-done(((f32[3,3,256,256]{3,2,1,0:T(8,128)}, f32[3,256,256]{2,1,0:T(8,128)}, f32[256,512]{1,0:T(8,128)}), (f32[3,3,256,256]{3,2,1,0:T(8,128)}, f32[3,256,256]{2,1,0:T(8,128)}, f32[256,512]{1,0:T(8,128)})) %all-reduce.8.cloned.1.call-update) | async-done | bytes 3670032 | tf_op jit(solution)/shard_map/psum | solution.py:107
  632.8 3.3 copy.37
  636.1 0.9 copy.38
  636.9 0.4 copy-done.19
  637.4 0.8 copy.39
  (95 shorter events, 5.2 us)
Async XLA Ops:
  7.2 54.2 %copy-start = (bf16[256,512]{1,0:T(8,128)(2,1)S(1)}, bf16[256,512]{1,0:T(8,128)(2,1)}, u32[]{:S(2)}) copy-start(bf16[256,512]{1,0:T(8,128)(2,1)} %param.9) | copy-start | bytes 786436
  7.2 351.9 %all-reduce.6.cloned.1.call-start = ((), (), s32[]{:S(2)}) async-start(), calls=%async_computation | async-start | bytes 2097152 | tf_op jit(solution)/shard_map/psum | solution.py:75
  13.6 10.1 %copy-start.5 = (bf16[784,256]{1,0:T(8,128)(2,1)}, bf16[784,256]{1,0:T(8,128)(2,1)S(1)}, u32[]{:S(2)}) copy-start(bf16[784,256]{1,0:T(8,128)(2,1)S(1)} %reshape.210) | copy-start | bytes 1204228
  14.0 7.5 %copy-start.3 = (bf16[784,256]{1,0:T(8,128)(2,1)}, bf16[784,256]{1,0:T(8,128)(2,1)S(1)}, u32[]{:S(2)}) copy-start(bf16[784,256]{1,0:T(8,128)(2,1)S(1)} %reshape.206) | copy-start | bytes 1204228
  14.2 7.6 %copy-start.7 = (bf16[784,256]{1,0:T(8,128)(2,1)}, bf16[784,256]{1,0:T(8,128)(2,1)S(1)}, u32[]{:S(2)}) copy-start(bf16[784,256]{1,0:T(8,128)(2,1)S(1)} %reshape.207) | copy-start | bytes 1204228
  15.5 6.8 %copy-start.9 = (bf16[784,256]{1,0:T(8,128)(2,1)}, bf16[784,256]{1,0:T(8,128)(2,1)S(1)}, u32[]{:S(2)}) copy-start(bf16[784,256]{1,0:T(8,128)(2,1)S(1)} %reshape.208) | copy-start | bytes 1204228
  19.8 1.8 copy-start.13
  19.8 1.5 copy-start.15
  22.4 1.0 copy-start.11
  23.7 1.0 copy-start.20
  25.9 5.5 copy-start.1
  26.0 7.7 %copy-start.27 = (s32[1,4]{1,0:T(1,128)S(1)}, s32[1,4]{1,0:T(1,128)}, u32[]{:S(2)}) copy-start(s32[1,4]{1,0:T(1,128)} %param.11) | copy-start | bytes 52
  26.0 7.7 %collective-permute-start = (bf16[1,1,14,14,256]{4,3,2,1,0:T(8,128)(2,1)S(1)}, bf16[1,1,14,14,256]{4,3,2,1,0:T(8,128)(2,1)S(1)}, u32[]{:S(2)}, u32[]{:S(2)}) collective-permute-start(bf16[1,1,14,14,256]{4,3,2,1,0:T(8,128)(2,1)S(1)} %get-tuple-element.17), channel_id=1, source_target_pairs={{0,1},{1,2},{2,3},{3,4},{4,5},{5,6},{6,7},{8,9},{9,10},{10,11},{11... | collective-permute-start | bytes 301064 | tf_op jit(solution)/shard_map/ppermute | solution.py:14
  30.1 5.6 collective-permute-start.1
  37.7 1.3 copy-start.17
  37.7 1.3 copy-start.22
  105.6 2.1 copy-start.23
  111.4 6.6 %copy-start.25 = (f32[1,256,256]{2,1,0:T(8,128)S(1)}, f32[1,256,256]{2,1,0:T(8,128)}, u32[]{:S(2)}) copy-start(f32[1,256,256]{2,1,0:T(8,128)} %convolution_bitcast_fusion) | copy-start | bytes 786436
  111.4 6.6 %copy-start.26 = (f32[1,256,256]{2,1,0:T(8,128)S(1)}, f32[1,256,256]{2,1,0:T(8,128)}, u32[]{:S(2)}) copy-start(f32[1,256,256]{2,1,0:T(8,128)} %convolution_bitcast_fusion.1) | copy-start | bytes 786436
  111.5 7.5 %collective-permute-start.2 = (bf16[1,1,14,14,256]{4,3,2,1,0:T(8,128)(2,1)S(1)}, bf16[1,1,14,14,256]{4,3,2,1,0:T(8,128)(2,1)S(1)}, u32[]{:S(2)}, u32[]{:S(2)}) collective-permute-start(bf16[1,1,14,14,256]{4,3,2,1,0:T(8,128)(2,1)S(1)} %get-tuple-element.13), channel_id=1, source_target_pairs={{1,0},{2,1},{3,2},{4,3},{5,4},{6,5},{7,6},{9,8},{10,9},{11,10},{12... | collective-permute-start | bytes 301064 | tf_op jit(solution)/shard_map/ppermute | solution.py:17
  112.9 6.1 collective-permute-start.3
  117.8 515.0 %all-reduce.8.cloned.1.call-start = ((), (), s32[]{:S(2)}) async-start(), calls=%async_computation.1 | async-start | bytes 7340032 | tf_op jit(solution)/shard_map/psum | solution.py:107
  120.0 1.5 copy-start.16
  120.1 1.4 copy-start.24
  120.1 1.5 copy-start.28
  121.6 1.5 copy-start.21
  121.6 1.9 copy-start.6
  123.1 1.0 copy-start.12
  123.5 1.0 copy-start.10
  124.8 1.0 copy-start.8
  125.2 1.0 copy-start.4
  126.2 1.0 copy-start.14
  359.1 1.6 copy-start.2
  632.8 3.3 copy-start.18
  636.1 1.3 copy-start.19
Sparse Core Ops, SparseCore 0:
  117.9 241.1 all-reduce.5
  366.4 266.2 all-reduce.7
where the time goes:
time: 647 us; the launch traced here: 645 us
  waiting for transfers between devices  503 us (78%)
  blocking collectives  56 us (9%)
  local copies, waits for them, and re-layouts  23.1 us (4%)
  matrix products  22.6 us (3%)
  between operations  15.4 us (2%)
  other arithmetic  14.3 us (2%)
  starting transfers between devices  11 us (2%)
    psum x1, waiting for transfers between devices, body(): lax.psum((spatial_term, temporal_term, proj_term), ('wide', 'tm'))  271 us
    psum x1, waiting for transfers between devices, body(): g_phat = lax.psum(16.0 * jnp.dot(g_s.T, zhat, precision=HI), 'wide')  230 us
    psum x1, blocking collectives, body(): pooled = lax.psum(pooled_loc, 'tm')  20.1 us
    psum x1, blocking collectives, body(): g_zhat = lax.psum(16.0 * jnp.dot(g_s, phat, precision=HI), 'tm')  19.7 us
    psum x1, blocking collectives, body(): lax.psum((jnp.sum(expo, axis=1, keepdims=True), jnp.sum(pos_expo, axis=1,...  16.2 us
  transfers between devices with their start and end apart: 6, of which 3 were waited for; matrix products, arithmetic and copies ran while one was open for 2% of the time, Pallas kernels for 0%

commit v1 on v0

v1 whole, which is shorter than its diff:
```python
import functools

import jax
import jax.numpy as jnp
from jax import lax
from jax.experimental import pallas as pl
from jax.experimental.pallas import tpu as pltpu
from jax.sharding import PartitionSpec as P

MESH = pl.DeviceIdType.MESH
F32 = jnp.float32
BF16 = jnp.bfloat16
HI = lax.Precision.HIGHEST

X_LO = 2
X_HI = 2
CORES = 2
LINE = 16

HALO, DHALO, POOL, AB, HEAD, PAIR, ZHEAD, CORE, XY, ZSUM, ZALL, XYALL, COREALL, SEMS = (
    0, 2, 4, 5, 6, 7, 8, 9, 13, 17, 18, 19, 23, 27
)


def dot(left, right):
    return jnp.dot(left, right, preferred_element_type=F32)


def sigmoid(v):
    return 1.0 / (1.0 + jnp.exp(-v))


def dsilu(v):
    sig = sigmoid(v)
    return sig * (1.0 + v * (1.0 - sig))


def same(n):
    return lax.broadcasted_iota(jnp.int32, (n, n), 0) == lax.broadcasted_iota(jnp.int32, (n, n), 1)


def to_column(row):
    return jnp.sum(jnp.where(same(row.shape[1]), row, 0.0), axis=1, keepdims=True)


def to_row(column):
    return jnp.sum(jnp.where(same(column.shape[0]), column, 0.0), axis=0, keepdims=True)


def step_kernel(
    sizes,
    x_ref, ws_ref, wt_ref, wp_ref, pr_ref, pos_ref,
    ag_ref, gproj_ref, gprm_ref,
    xs_ref, pre_ref, act_ref, dt_ref, dsend_ref, dhalo_ref, gt_ref, gs_ref, xt_ref, actt_ref, wtt_ref,
    ph_ref, pool_ref, ab_ref, wg_ref, gbuf_ref, rbuf_ref, cs_ref, xyr_ref, zsrc_ref, zr_ref, zred_ref, zg_ref,
    snd, rcv,
):
    n_wide, n_tm, frames, side, chan, embed, shard = sizes
    rows = side * LINE
    n_z = n_wide // (X_LO * CORES)
    n_y = n_tm // X_HI
    n_x = X_HI * X_LO
    n_xy = n_x * n_y

    wide = lax.axis_index("wide")
    tm = lax.axis_index("tm")
    core = wide % CORES
    x_lo = (wide // CORES) % X_LO
    z = wide // (CORES * X_LO)
    y = tm % n_y
    x = (tm // n_y) * X_LO + x_lo
    mine = x * n_y + y

    def xy_partner(d):
        px = (x + d // n_y) % n_x
        py = (y + d % n_y) % n_y
        return px * n_y + py, (z * (CORES * X_LO) + (px % X_LO) * CORES + core, (px // X_LO) * n_y + py)

    def z_partner(d):
        pz = (z + d) % n_z
        return pz, (pz * (CORES * X_LO) + x_lo * CORES + core, tm)

    sibling = (wide + 1 - 2 * core, tm)
    pair = (wide + (1 - 2 * x_lo) * CORES, tm)

    def send(src, dst, sem, device):
        copy = pltpu.make_async_remote_copy(
            src_ref=src, dst_ref=dst, send_sem=snd.at[sem], recv_sem=rcv.at[sem], device_id=device, device_id_type=MESH
        )
        copy.start()
        return copy

    def drain(ref, sem):
        pltpu.make_async_copy(ref, ref, sem).wait()

    barrier = pltpu.get_barrier_semaphore()

    def greet_xy(d, carry):
        pl.semaphore_signal(barrier, inc=1, device_id=xy_partner(d)[1], device_id_type=MESH)
        return carry

    def greet_z(d, carry):
        pl.semaphore_signal(barrier, inc=1, device_id=z_partner(d)[1], device_id_type=MESH)
        return carry

    lax.fori_loop(1, n_xy, greet_xy, 0)
    lax.fori_loop(1, n_z, greet_z, 0)
    pl.semaphore_signal(barrier, inc=1, device_id=sibling, device_id_type=MESH)

    row_id = lax.broadcasted_iota(jnp.int32, (rows, chan), 0)
    inside = (row_id % LINE) < side
    low_mask = jnp.where(tm > 0, 1.0, 0.0).astype(F32)
    high_mask = jnp.where(tm < n_tm - 1, 1.0, 0.0).astype(F32)
    full = LINE * (side + 2)

    def shifted(ref, f):
        flat = ref[1, f].reshape(full, chan).astype(F32)
        ahead = pltpu.roll(flat, 1, 0).astype(BF16).reshape(side + 2, LINE, chan)
        behind = pltpu.roll(flat, full - 1, 0).astype(BF16).reshape(side + 2, LINE, chan)
        return ahead, behind

    def conv(f):
        xs_ref[1, f] = jnp.zeros((side + 2, LINE, chan), BF16)
        xs_ref[1, f, 1 : side + 1, 0:side, :] = x_ref[0, f]
        ahead, behind = shifted(xs_ref, f)
        xs_ref[0, f] = ahead
        xs_ref[2, f] = behind
        total = jnp.zeros((rows, chan), F32)
        for a in range(3):
            for b in range(3):
                total = total + dot(xs_ref[b, f, a : a + side].reshape(rows, chan), ws_ref[3 * a + b])
        pre_ref[f] = total
        act_ref[f + 1] = jnp.where(inside, total * sigmoid(total), 0.0).astype(BF16)

    left = (wide, (tm + n_tm - 1) % n_tm)
    right = (wide, (tm + 1) % n_tm)

    conv(0)
    conv(frames - 1)
    pl.semaphore_wait(barrier, n_xy - 1 + n_z - 1 + 1)
    to_left = send(act_ref.at[1], act_ref.at[frames + 1], HALO + 1, left)
    to_right = send(act_ref.at[frames], act_ref.at[0], HALO, right)
    for f in range(1, frames - 1):
        conv(f)
    p32 = pr_ref[...].astype(F32)
    pnorm = jnp.sqrt(jnp.sum(p32 * p32, axis=1, keepdims=True) + 1e-06)
    ph_ref[...] = p32 / pnorm

    pooled8 = jnp.zeros((8, chan), F32)
    for f in range(frames):
        pooled8 = pooled8 + jnp.sum(
            xs_ref[1, f, 1 : side + 1].reshape(rows // 8, 8, chan).astype(F32), axis=0
        )
    to_right.wait_recv()
    to_left.wait_recv()
    for f in list(range(1, frames - 1)) + [0, frames - 1]:
        below = dot(act_ref[f], wt_ref[0])
        above = dot(act_ref[f + 2], wt_ref[2])
        if f == 0:
            below = below * low_mask
        if f == frames - 1:
            above = above * high_mask
        pre = below + dot(act_ref[f + 1], wt_ref[1]) + above
        sig = sigmoid(pre)
        pooled8 = pooled8 + jnp.sum((pre * sig).reshape(rows // 8, 8, chan), axis=0)
        dt_ref[f] = jnp.where(inside, sig * (1.0 + pre * (1.0 - sig)), 0.0)
    pool_ref[tm] = pooled8

    def tm_partner(d):
        return (wide, (tm + d) % n_tm)

    def send_pool(d, carry):
        send(pool_ref.at[tm], pool_ref.at[tm], POOL, tm_partner(d))
        return carry

    lax.fori_loop(1, n_tm, send_pool, 0)

    dsend_ref[0] = dt_ref[0].astype(BF16)
    dsend_ref[1] = dt_ref[frames - 1].astype(BF16)
    d_left = send(dsend_ref.at[0], dhalo_ref.at[1], DHALO + 1, left)
    d_right = send(dsend_ref.at[1], dhalo_ref.at[0], DHALO, right)
    for f in range(frames):
        pre_ref[f] = dsilu(pre_ref[f])
        xt_ref[:, f * rows : (f + 1) * rows] = xs_ref[1, f, 1 : side + 1].reshape(rows, chan).T
        actt_ref[:, f * rows : (f + 1) * rows] = act_ref[f + 1].T
        for b in range(3):
            gs_ref[b, f, 0] = jnp.zeros((LINE, chan), BF16)
            gs_ref[b, f, side + 1] = jnp.zeros((LINE, chan), BF16)
    for t in range(3):
        wtt_ref[t] = wt_ref[t].T
    wp = wp_ref[...].astype(F32)
    ids = lax.broadcasted_iota(jnp.int32, (shard, 1), 0) + tm * shard
    multi = jnp.zeros((shard, 1), F32)
    for k in range(pos_ref.shape[1]):
        multi = multi + jnp.where(ids == pos_ref[0, k], 1.0, 0.0)

    drain(pool_ref.at[0 : n_tm - 1], rcv.at[POOL])
    pooled = jnp.sum(jnp.sum(pool_ref[...], axis=0), axis=0, keepdims=True)
    zrow = jnp.sum(wp * to_column(pooled), axis=0, keepdims=True)
    znorm = jnp.sqrt(jnp.sum(zrow * zrow, axis=1, keepdims=True) + 1e-06)
    zhat = zrow / znorm
    expo = jnp.exp(16.0 * jnp.sum(ph_ref[...] * zhat, axis=1, keepdims=True))
    hits = multi * expo
    part_a = jnp.sum(ph_ref[...] * expo, axis=0, keepdims=True)
    part_b = jnp.sum(ph_ref[...] * hits, axis=0, keepdims=True)
    tiles = embed // 128
    for k in range(tiles):
        ab_ref[tm, 0, k : k + 1, :] = part_a[:, 128 * k : 128 * (k + 1)]
        ab_ref[tm, 0, tiles + k : tiles + k + 1, :] = part_b[:, 128 * k : 128 * (k + 1)]
    ab_ref[tm, 1, 0:4, :] = jnp.broadcast_to(jnp.sum(expo, axis=0, keepdims=True), (4, 128))
    ab_ref[tm, 1, 4:8, :] = jnp.broadcast_to(jnp.sum(hits, axis=0, keepdims=True), (4, 128))

    def send_ab(d, carry):
        send(ab_ref.at[tm], ab_ref.at[tm], AB, tm_partner(d))
        return carry

    lax.fori_loop(1, n_tm, send_ab, 0)
    drain(ab_ref.at[0 : n_tm - 1], rcv.at[AB])
    summed = jnp.sum(ab_ref[...], axis=0)
    sum_a = jnp.concatenate([summed[0, k : k + 1] for k in range(tiles)], axis=1)
    sum_b = jnp.concatenate([summed[0, tiles + k : tiles + k + 1] for k in range(tiles)], axis=1)
    total = summed[1, 0:1, 0:1]
    pos_total = summed[1, 4:5, 0:1]
    g_zhat = 16.0 * (sum_a / total - sum_b / pos_total)
    g_z = (g_zhat - zhat * jnp.sum(zhat * g_zhat, axis=1, keepdims=True)) / znorm
    g_pooled = to_row(jnp.sum(wp * g_z, axis=1, keepdims=True))
    g_s = expo / total - hits / pos_total

    for k in range(chan // 128):
        wg_ref[wide, k : k + 1, :] = pooled[:, 128 * k : 128 * (k + 1)]
    for k in range(tiles):
        wg_ref[wide, 2 + k : 3 + k, :] = g_z[:, 128 * k : 128 * (k + 1)]
        wg_ref[wide, 6 + k : 7 + k, :] = zhat[:, 128 * k : 128 * (k + 1)]
        wg_ref[wide, 10 + k : 11 + k, :] = to_row(g_s[128 * k : 128 * (k + 1)])
    wg_ref[wide, 14:16, :] = jnp.zeros((2, 128), F32)
    head_copy = send(wg_ref.at[wide], wg_ref.at[wide], HEAD, sibling)

    for f in range(frames):
        gt_ref[f + 1] = (dt_ref[f] * g_pooled).astype(BF16)
    d_right.wait_recv()
    d_left.wait_recv()
    gt_ref[0] = (dhalo_ref[0].astype(F32) * (g_pooled * low_mask)).astype(BF16)
    gt_ref[frames + 1] = (dhalo_ref[1].astype(F32) * (g_pooled * high_mask)).astype(BF16)

    half = chan // 2
    core_copies = []

    def put(g, t, grad):
        gbuf_ref[g, 0, t] = grad[:half]
        gbuf_ref[g, 1, t] = grad[half:]

    def send_core(g):
        core_copies.append(send(gbuf_ref.at[g, 1 - core], rbuf_ref.at[g], CORE + g, sibling))

    def send_xy(g):
        core_copies[g].wait_recv()
        for t in range(3):
            both = (gbuf_ref[g, core, t] + rbuf_ref[g, t]).astype(BF16)
            for p in range(n_xy):
                i, j = p // 2, p % 2
                cs_ref[g, p, t] = both[16 * i : 16 * (i + 1), 128 * j : 128 * (j + 1)]

        def one(d, carry):
            p, device = xy_partner(d)
            send(cs_ref.at[g, p], xyr_ref.at[g, d - 1], XY + g, device)
            return carry

        lax.fori_loop(1, n_xy, one, 0)

    for t in range(3):
        put(0, t, dot(actt_ref[...], gt_ref[2 - t : 2 - t + frames].reshape(frames * rows, chan)))
    send_core(0)

    for f in range(frames):
        g_act = jnp.zeros((rows, chan), F32)
        for t in range(3):
            g_act = g_act + dot(gt_ref[f + 2 - t], wtt_ref[t])
        gs_ref[1, f, 1 : side + 1] = (g_act * pre_ref[f]).astype(BF16).reshape(side, LINE, chan)
        ahead, behind = shifted(gs_ref, f)
        gs_ref[2, f] = ahead
        gs_ref[0, f] = behind
    send_xy(0)
    head_copy.wait_recv()
    pair_rows = wg_ref.at[pl.ds(wide - core, CORES)]
    pair_copy = send(pair_rows, pair_rows, PAIR, pair)

    for a in range(3):
        for b in range(3):
            window = gs_ref[b, :, 2 - a : 2 - a + side].reshape(frames * rows, chan)
            put(1 + a, b, dot(xt_ref[...], window))
        send_core(1 + a)
        if a == 0:
            pair_copy.wait_recv()
            z_rows = wg_ref.at[pl.ds(z * (CORES * X_LO), CORES * X_LO)]

            def send_head(d, carry):
                send(z_rows, z_rows, ZHEAD, z_partner(d)[1])
                return carry

            lax.fori_loop(1, n_z, send_head, 0)
        if a > 0:
            send_xy(a)
    send_xy(3)

    drain(wg_ref.at[0 : n_wide - CORES * X_LO], rcv.at[ZHEAD])

    def all_clips(first, count):
        return jnp.concatenate([wg_ref[:, first + k, :] for k in range(count)], axis=1)

    over_clips = (((0,), (0,)), ((), ()))
    pooled_all = all_clips(0, chan // 128)
    g_z_all = all_clips(2, tiles)
    zhat_all = all_clips(6, tiles)
    g_s_all = all_clips(10, shard // 128)
    gproj_ref[...] = lax.dot_general(pooled_all, g_z_all, over_clips, precision=HI, preferred_element_type=F32)
    g_phat = 16.0 * lax.dot_general(g_s_all, zhat_all, over_clips, precision=HI, preferred_element_type=F32)
    phat = ph_ref[...]
    p32 = pr_ref[...].astype(F32)
    pnorm = jnp.sqrt(jnp.sum(p32 * p32, axis=1, keepdims=True) + 1e-06)
    gprm_ref[...] = (g_phat - phat * jnp.sum(phat * g_phat, axis=1, keepdims=True)) / pnorm

    for g in range(4):
        drain(xyr_ref.at[g], rcv.at[XY + g])
        value = cs_ref[g, mine].astype(F32)
        for d in range(n_xy - 1):
            value = value + xyr_ref[g, d].astype(F32)
        for t in range(3):
            zsrc_ref[6 * g + 2 * t] = value[t, :8]
            zsrc_ref[6 * g + 2 * t + 1] = value[t, 8:]
    chunk = 24 // n_z

    def send_zsum(d, carry):
        pz, device = z_partner(d)
        send(zsrc_ref.at[pl.ds(pz * chunk, chunk)], zr_ref.at[d - 1], ZSUM, device)
        return carry

    lax.fori_loop(1, n_z, send_zsum, 0)
    drain(zr_ref, rcv.at[ZSUM])
    own = pl.ds(z * chunk, chunk)
    reduced = zsrc_ref[own] + jnp.sum(zr_ref[...], axis=0)
    zred_ref[...] = reduced
    zg_ref[own] = reduced

    def send_zall(d, carry):
        send(zred_ref, zg_ref.at[own], ZALL, z_partner(d)[1])
        return carry

    lax.fori_loop(1, n_z, send_zall, 0)
    drain(zg_ref.at[0 : 24 - chunk], rcv.at[ZALL])
    for q in range(12):
        ag_ref[core, mine, q] = jnp.concatenate([zg_ref[2 * q], zg_ref[2 * q + 1]], axis=0).astype(BF16)
    own_piece = ag_ref.at[core, mine]
    for dx in (0, 1, 3, 2):

        def send_piece(dy, carry):
            send(own_piece, own_piece, XYALL + dx, xy_partner(dx * n_y + dy)[1])
            return carry

        lax.fori_loop(1 if dx == 0 else 0, n_y, send_piece, 0)
    last = []
    for dx in (0, 1, 3, 2):
        count = n_y - 1 if dx == 0 else n_y
        drain(ag_ref.at[0, 0:count], rcv.at[XYALL + dx])
        column = ag_ref.at[core, pl.ds(((x + n_x - dx) % n_x) * n_y, n_y)]
        last.append(send(column, column, COREALL + dx, sibling))
    for copy in last:
        copy.wait_recv()

    for copy in [to_left, to_right, d_left, d_right, head_copy, pair_copy] + core_copies + last:
        copy.wait_send()
    drain(pool_ref.at[0 : n_tm - 1], snd.at[POOL])
    drain(ab_ref.at[0 : n_tm - 1], snd.at[AB])
    drain(wg_ref.at[0 : n_wide - CORES * X_LO], snd.at[ZHEAD])
    for g in range(4):
        drain(xyr_ref.at[g], snd.at[XY + g])
    drain(zr_ref, snd.at[ZSUM])
    drain(zg_ref.at[0 : 24 - chunk], snd.at[ZALL])
    for dx in range(n_x):
        drain(ag_ref.at[0, 0 : n_y - 1 if dx == 0 else n_y], snd.at[XYALL + dx])


def lay_kernel(ag_ref, gproj_ref, gprm_ref, gs_out, gt_out, gproj_out, gprm_out, buf_ref, sems):
    copies = [
        pltpu.make_async_copy(gprm_ref, gprm_out, sems.at[12]),
        pltpu.make_async_copy(gproj_ref, gproj_out, sems.at[13]),
    ]
    for copy in copies:
        copy.start()
    cores, pieces, taps = ag_ref.shape[:3]
    half = buf_ref.shape[1] // cores
    for q in range(taps):
        for c in range(cores):
            for p in range(pieces):
                i, j = p // 2, p % 2
                r = half * c + 16 * i
                buf_ref[q, r : r + 16, 128 * j : 128 * (j + 1)] = ag_ref[c, p, q].astype(F32)
        target = gt_out.at[q] if q < 3 else gs_out.at[q - 3]
        copies.append(pltpu.make_async_copy(buf_ref.at[q], target, sems.at[q]))
        copies[-1].start()
    for copy in copies:
        copy.wait()


def body(clips_in, w_spatial, w_temporal, w_proj, prompts, positives):
    n_wide, n_tm = lax.axis_size("wide"), lax.axis_size("tm")
    clips, frames, side, _, chan = clips_in.shape
    shard, embed = prompts.shape
    rows = side * LINE
    n_z = n_wide // (X_LO * CORES)
    n_xy = X_HI * X_LO * (n_tm // X_HI)
    sizes = (n_wide, n_tm, frames, side, chan, embed, shard)
    vmem = pl.BlockSpec(memory_space=pltpu.VMEM)
    smem = pl.BlockSpec(memory_space=pltpu.SMEM)
    half = chan // 2
    gathered, grad_proj, grad_prompts = pl.pallas_call(
        functools.partial(step_kernel, sizes),
        out_shape=(
            jax.ShapeDtypeStruct((CORES, n_xy, 12, 16, 128), BF16),
            jax.ShapeDtypeStruct((chan, embed), F32),
            jax.ShapeDtypeStruct((shard, embed), F32),
        ),
        in_specs=[vmem] * 5 + [smem],
        out_specs=(vmem, vmem, vmem),
        scratch_shapes=[
            pltpu.VMEM((3, frames, side + 2, LINE, chan), BF16),
            pltpu.VMEM((frames, rows, chan), F32),
            pltpu.VMEM((frames + 2, rows, chan), BF16),
            pltpu.VMEM((frames, rows, chan), F32),
            pltpu.VMEM((2, rows, chan), BF16),
            pltpu.VMEM((2, rows, chan), BF16),
            pltpu.VMEM((frames + 2, rows, chan), BF16),
            pltpu.VMEM((3, frames, side + 2, LINE, chan), BF16),
            pltpu.VMEM((chan, frames * rows), BF16),
            pltpu.VMEM((chan, frames * rows), BF16),
            pltpu.VMEM((3, chan, chan), BF16),
            pltpu.VMEM((shard, embed), F32),
            pltpu.VMEM((n_tm, 8, chan), F32),
            pltpu.VMEM((n_tm, 2, 8, 128), F32),
            pltpu.VMEM((n_wide, 16, 128), F32),
            pltpu.VMEM((4, 2, 3, half, chan), F32),
            pltpu.VMEM((4, 3, half, chan), F32),
            pltpu.VMEM((4, n_xy, 3, 16, 128), BF16),
            pltpu.VMEM((4, n_xy - 1, 3, 16, 128), BF16),
            pltpu.VMEM((24, 8, 128), F32),
            pltpu.VMEM((n_z - 1, 24 // n_z, 8, 128), F32),
            pltpu.VMEM((24 // n_z, 8, 128), F32),
            pltpu.VMEM((24, 8, 128), F32),
            pltpu.SemaphoreType.DMA((SEMS,)),
            pltpu.SemaphoreType.DMA((SEMS,)),
        ],
        compiler_params=pltpu.CompilerParams(
            collective_id=0, has_side_effects=True, vmem_limit_bytes=48 * 1024 * 1024
        ),
        name="step",
    )(clips_in, w_spatial.reshape(9, chan, chan), w_temporal, w_proj, prompts, positives)
    anywhere = pl.BlockSpec(memory_space=pl.ANY)
    grad_s, grad_t, grad_p, grad_m = pl.pallas_call(
        lay_kernel,
        out_shape=(
            jax.ShapeDtypeStruct((9, chan, chan), F32),
            jax.ShapeDtypeStruct((3, chan, chan), F32),
            jax.ShapeDtypeStruct((chan, embed), F32),
            jax.ShapeDtypeStruct((shard, embed), F32),
        ),
        in_specs=[vmem] * 3,
        out_specs=(anywhere,) * 4,
        scratch_shapes=[pltpu.VMEM((12, chan, chan), F32), pltpu.SemaphoreType.DMA((14,))],
        name="lay_out",
    )(gathered, grad_proj, grad_prompts)
    return grad_s.reshape(3, 3, chan, chan), grad_t, grad_p, grad_m


def solution(mesh):
    placed = (P("wide", "tm", None, None, None), P(), P(), P(), P("tm", None), P("wide", None))
    return jax.shard_map(
        body, mesh=mesh, in_specs=placed, out_specs=(P(), P(), P(), P("tm", None)), check_vma=False
    )
```

time: 647 us -> 81.7 us (0.13)
  waiting for transfers between devices: 503 us -> 0 us
  Pallas kernels: 0 us -> 71.9 us
  blocking collectives: 56 us -> 0 us
  matrix products: 22.6 us -> 0 us
  between operations: 15.4 us -> 0.66 us
  other arithmetic: 14.3 us -> 0 us
  local copies, waits for them, and re-layouts: 23.1 us -> 8.87 us
  starting transfers between devices: 11 us -> 0 us
    psum x2 -> x0, waiting for transfers between devices: 501 us -> none  [the longest x1 271 us: body(): lax.psum((spatial_term, temporal_term, proj_term), ('wide', 'tm'))]
    pallas_call x0 -> x2, Pallas kernels: none -> 71.9 us  [the longest x1 67.8 us: body(): pl.pallas_call(functools.partial(step_kernel, sizes), out_shape=(jax.Shap...]
    psum x3 -> x0, blocking collectives: 56 us -> none  [the longest x1 20.1 us: body(): pooled = lax.psum(pooled_loc, 'tm')]
    dot_general x31 -> x0, matrix products: 22.6 us -> none  [the longest x12 5.61 us: contract(): lax.dot_general(left, right, (((0,), (0,)), ((), ())), preferred_element_...]
    ppermute x4 -> x0, starting transfers between devices: 10.8 us -> none  [the longest x2 8.03 us: extended(): lax.ppermute(lax.slice_in_dim(block, block.shape[dim] - width, None, axis...]
    slice x11 -> x0, local copies, waits for them, and re-layouts: 8.76 us -> none  [the longest x8 8.67 us: body(): window = padded[:, :, a:a + side, b:b + side, :].reshape(rows, chan)]
  transfers between devices with their start and end apart: 6 -> 0, of which waited for: 3 -> 0; matrix products, arithmetic and copies ran while one was open for 2% -> 0% of each run, Pallas kernels for 0% -> 0%
where the time goes in v1:
time: 81.7 us; the launch traced here: 81.4 us
  Pallas kernels  71.9 us (88%)
  local copies, waits for them, and re-layouts  8.87 us (11%)
    pallas_call x1, Pallas kernels, body(): pl.pallas_call(functools.partial(step_kernel, sizes), out_shape=(jax.Shap...  67.8 us
    unnamed x17, local copies, waits for them, and re-layouts  8.87 us
    pallas_call x1, Pallas kernels, body(): pl.pallas_call(lay_kernel, out_shape=(jax.ShapeDtypeStruct((9, chan, chan...  4.14 us

profile of v1, /device:TPU:1, one launch (start us, length us, event | category | flops | bytes accessed | tf_op | source)
XLA Modules:
  0.0 81.4 jit_solution(13654345886686062725)
XLA Ops:
  0.6 1.1 %copy.10.x_ref = bf16[1,4,14,14,256]{4,3,2,1,0:T(8,128)(2,1)S(1)} copy(bf16[1,4,14,14,256]{4,1,3,2,0:T(4,128)(2,1)} %param.6) | data formatting | bytes 802816 | tf_op args[0]
  1.7 0.0 copy-start.1
  1.7 1.3 %copy-done.1 = bf16[3,3,256,256]{3,2,1,0:T(8,128)(2,1)S(1)} copy-done((bf16[3,3,256,256]{3,2,1,0:T(8,128)(2,1)S(1)}, bf16[3,3,256,256]{3,2,1,0:T(8,128)(2,1)}, u32[]{:S(2)}) %copy-start.1) | copy-done | bytes 1179672
  3.0 0.0 copy-start.3
  3.0 1.0 %copy-done.3 = bf16[512,512]{1,0:T(8,128)(2,1)S(1)} copy-done((bf16[512,512]{1,0:T(8,128)(2,1)S(1)}, bf16[512,512]{1,0:T(8,128)(2,1)}, u32[]{:S(2)}) %copy-start.3) | copy-done | bytes 524312
  4.0 0.0 copy-start.5
  4.0 1.0 %copy-done.5 = bf16[3,256,256]{2,1,0:T(8,128)(2,1)S(1)} copy-done((bf16[3,256,256]{2,1,0:T(8,128)(2,1)S(1)}, bf16[3,256,256]{2,1,0:T(8,128)(2,1)}, u32[]{:S(2)}) %copy-start.5) | copy-done | bytes 393240
  5.0 0.0 copy-start.6
  5.0 0.9 %copy-done.6 = bf16[256,512]{1,0:T(8,128)(2,1)S(1)} copy-done((bf16[256,512]{1,0:T(8,128)(2,1)S(1)}, bf16[256,512]{1,0:T(8,128)(2,1)}, u32[]{:S(2)}) %copy-start.6) | copy-done | bytes 262168
  6.0 0.0 copy-start.7
  6.0 0.7 copy-done.7
  6.6 67.8 %step.1 = (bf16[2,16,12,16,128]{4,3,2,1,0:T(8,128)(2,1)S(1)}, f32[256,512]{1,0:T(8,128)S(1)}, f32[512,512]{1,0:T(8,128)S(1)}) custom-call(bf16[1,4,14,14,256]{4,3,2,1,0:T(8,128)(2,1)S(1)} %copy.10.x_ref, bf16[9,256,256]{2,1,0:T(8,128)(2,1)S(1)} %bitcast.2, bf16[3,256,256]{2,1,0:T(8,128)(2,1)S(1)} %copy-done.5, bf16[256,512]{1,0:T(8,128)(2,1)S(1)} %copy-done.6, ...), custom_call_target="tpu_custom_call" | custom-call | tf_op jit(solution)/shard_map/step/pallas_call | solution.py:415
  74.4 0.0 copy-start
  74.4 1.1 %copy-done = bf16[2,16,12,16,128]{4,3,2,1,0:T(8,128)(2,1)} copy-done((bf16[2,16,12,16,128]{4,3,2,1,0:T(8,128)(2,1)}, bf16[2,16,12,16,128]{4,3,2,1,0:T(8,128)(2,1)S(1)}, u32[]{:S(2)}) %copy-start) | copy-done | bytes 1572888
  75.5 0.0 copy-start.2
  75.5 1.0 %copy-done.2 = f32[512,512]{1,0:T(8,128)} copy-done((f32[512,512]{1,0:T(8,128)}, f32[512,512]{1,0:T(8,128)S(1)}, u32[]{:S(2)}) %copy-start.2) | copy-done | bytes 1048600
  76.5 0.0 copy-start.4
  76.5 0.8 copy-done.4
  77.3 4.1 %lay_out.1 = (f32[9,256,256]{2,1,0:T(8,128)}, f32[3,256,256]{2,1,0:T(8,128)}, f32[256,512]{1,0:T(8,128)}, f32[512,512]{1,0:T(8,128)}) custom-call(bf16[2,16,12,16,128]{4,3,2,1,0:T(8,128)(2,1)} %copy-done, f32[256,512]{1,0:T(8,128)} %copy-done.4, f32[512,512]{1,0:T(8,128)} %copy-done.2), custom_call_target="tpu_custom_call" | custom-call | tf_op jit(solution)/shard_map/lay_out/pallas_call | solution.py:457
Async XLA Ops:
  1.7 1.3 %copy-start.1 = (bf16[3,3,256,256]{3,2,1,0:T(8,128)(2,1)S(1)}, bf16[3,3,256,256]{3,2,1,0:T(8,128)(2,1)}, u32[]{:S(2)}) copy-start(bf16[3,3,256,256]{3,2,1,0:T(8,128)(2,1)} %param.7) | copy-start | bytes 3538948
  3.0 1.0 %copy-start.3 = (bf16[512,512]{1,0:T(8,128)(2,1)S(1)}, bf16[512,512]{1,0:T(8,128)(2,1)}, u32[]{:S(2)}) copy-start(bf16[512,512]{1,0:T(8,128)(2,1)} %pr_ref.1) | copy-start | bytes 1572868
  4.0 1.0 %copy-start.5 = (bf16[3,256,256]{2,1,0:T(8,128)(2,1)S(1)}, bf16[3,256,256]{2,1,0:T(8,128)(2,1)}, u32[]{:S(2)}) copy-start(bf16[3,256,256]{2,1,0:T(8,128)(2,1)} %wt_ref.1) | copy-start | bytes 1179652
  5.0 0.9 %copy-start.6 = (bf16[256,512]{1,0:T(8,128)(2,1)S(1)}, bf16[256,512]{1,0:T(8,128)(2,1)}, u32[]{:S(2)}) copy-start(bf16[256,512]{1,0:T(8,128)(2,1)} %wp_ref.1) | copy-start | bytes 786436
  6.0 0.7 copy-start.7
  74.4 1.1 %copy-start = (bf16[2,16,12,16,128]{4,3,2,1,0:T(8,128)(2,1)}, bf16[2,16,12,16,128]{4,3,2,1,0:T(8,128)(2,1)S(1)}, u32[]{:S(2)}) copy-start(bf16[2,16,12,16,128]{4,3,2,1,0:T(8,128)(2,1)S(1)} %get-tuple-element.11.ag_ref) | copy-start | bytes 4718596
  75.5 1.0 %copy-start.2 = (f32[512,512]{1,0:T(8,128)}, f32[512,512]{1,0:T(8,128)S(1)}, u32[]{:S(2)}) copy-start(f32[512,512]{1,0:T(8,128)S(1)} %get-tuple-element.13.gprm_ref) | copy-start | bytes 3145732
  76.5 0.8 copy-start.4

commit v2 on v1

--- a/solution.py
+++ b/solution.py
@@ -18,8 +18,10 @@
 LINE = 16
 
 HALO, DHALO, POOL, AB, HEAD, PAIR, ZHEAD, CORE, XY, ZSUM, ZALL, XYALL, COREALL, SEMS = (
-    0, 2, 4, 5, 6, 7, 8, 9, 13, 17, 18, 19, 23, 27
+    0, 2, 4, 5, 6, 7, 8, 9, 12, 15, 18, 21, 33, 45
 )
+GROUPS = 3
+TAPS = 4
 
 
 def dot(left, right):
@@ -49,11 +51,12 @@
 
 def step_kernel(
     sizes,
-    x_ref, ws_ref, wt_ref, wp_ref, pr_ref, pos_ref,
+    x_ref, ws_hbm, wt_hbm, wp_hbm, pr_hbm, pos_hbm,
     ag_ref, gproj_ref, gprm_ref,
     xs_ref, pre_ref, act_ref, dt_ref, dsend_ref, dhalo_ref, gt_ref, gs_ref, xt_ref, actt_ref, wtt_ref,
     ph_ref, pool_ref, ab_ref, wg_ref, gbuf_ref, rbuf_ref, cs_ref, xyr_ref, zsrc_ref, zr_ref, zred_ref, zg_ref,
-    snd, rcv,
+    ws_ref, wt_ref, wp_ref, pr_ref, pos_ref,
+    snd, rcv, loc,
 ):
     n_wide, n_tm, frames, side, chan, embed, shard = sizes
     rows = side * LINE
@@ -93,6 +96,16 @@
     def drain(ref, sem):
         pltpu.make_async_copy(ref, ref, sem).wait()
 
+    loads = [
+        pltpu.make_async_copy(src, dst, loc.at[i])
+        for i, (src, dst) in enumerate(
+            [(ws_hbm, ws_ref), (pr_hbm, pr_ref), (wt_hbm, wt_ref), (wp_hbm, wp_ref), (pos_hbm, pos_ref)]
+        )
+    ]
+    for load in loads:
+        load.start()
+    load_ws, load_pr, load_wt, load_wp, load_pos = loads
+
     barrier = pltpu.get_barrier_semaphore()
 
     def greet_xy(d, carry):
@@ -119,12 +132,14 @@
         behind = pltpu.roll(flat, full - 1, 0).astype(BF16).reshape(side + 2, LINE, chan)
         return ahead, behind
 
-    def conv(f):
+    def window(f):
         xs_ref[1, f] = jnp.zeros((side + 2, LINE, chan), BF16)
         xs_ref[1, f, 1 : side + 1, 0:side, :] = x_ref[0, f]
         ahead, behind = shifted(xs_ref, f)
         xs_ref[0, f] = ahead
         xs_ref[2, f] = behind
+
+    def conv(f):
         total = jnp.zeros((rows, chan), F32)
         for a in range(3):
             for b in range(3):
@@ -135,13 +150,18 @@
     left = (wide, (tm + n_tm - 1) % n_tm)
     right = (wide, (tm + 1) % n_tm)
 
+    window(0)
+    window(frames - 1)
+    load_ws.wait()
     conv(0)
     conv(frames - 1)
     pl.semaphore_wait(barrier, n_xy - 1 + n_z - 1 + 1)
     to_left = send(act_ref.at[1], act_ref.at[frames + 1], HALO + 1, left)
     to_right = send(act_ref.at[frames], act_ref.at[0], HALO, right)
     for f in range(1, frames - 1):
+        window(f)
         conv(f)
+    load_pr.wait()
     p32 = pr_ref[...].astype(F32)
     pnorm = jnp.sqrt(jnp.sum(p32 * p32, axis=1, keepdims=True) + 1e-06)
     ph_ref[...] = p32 / pnorm
@@ -151,6 +171,7 @@
         pooled8 = pooled8 + jnp.sum(
             xs_ref[1, f, 1 : side + 1].reshape(rows // 8, 8, chan).astype(F32), axis=0
         )
+    load_wt.wait()
     to_right.wait_recv()
     to_left.wait_recv()
     for f in list(range(1, frames - 1)) + [0, frames - 1]:
@@ -188,11 +209,13 @@
             gs_ref[b, f, side + 1] = jnp.zeros((LINE, chan), BF16)
     for t in range(3):
         wtt_ref[t] = wt_ref[t].T
+    load_wp.wait()
+    load_pos.wait()
     wp = wp_ref[...].astype(F32)
     ids = lax.broadcasted_iota(jnp.int32, (shard, 1), 0) + tm * shard
     multi = jnp.zeros((shard, 1), F32)
     for k in range(pos_ref.shape[1]):
-        multi = multi + jnp.where(ids == pos_ref[0, k], 1.0, 0.0)
+        multi = multi + jnp.where(ids == pos_ref[0:1, k : k + 1], 1.0, 0.0)
 
     drain(pool_ref.at[0 : n_tm - 1], rcv.at[POOL])
     pooled = jnp.sum(jnp.sum(pool_ref[...], axis=0), axis=0, keepdims=True)
@@ -245,7 +268,8 @@
     half = chan // 2
     core_copies = []
 
-    def put(g, t, grad):
+    def put(q, grad):
+        g, t = q // TAPS, q % TAPS
         gbuf_ref[g, 0, t] = grad[:half]
         gbuf_ref[g, 1, t] = grad[half:]
 
@@ -254,7 +278,7 @@
 
     def send_xy(g):
         core_copies[g].wait_recv()
-        for t in range(3):
+        for t in range(TAPS):
             both = (gbuf_ref[g, core, t] + rbuf_ref[g, t]).astype(BF16)
             for p in range(n_xy):
                 i, j = p // 2, p % 2
@@ -267,9 +291,62 @@
 
         lax.fori_loop(1, n_xy, one, 0)
 
+    def put_spatial(q):
+        a, b = (q - 3) // 3, (q - 3) % 3
+        put(q, dot(xt_ref[...], gs_ref[b, :, 2 - a : 2 - a + side].reshape(frames * rows, chan)))
+
+    def sum_z(g):
+        drain(xyr_ref.at[g], rcv.at[XY + g])
+        value = cs_ref[g, mine].astype(F32)
+        for d in range(n_xy - 1):
+            value = value + xyr_ref[g, d].astype(F32)
+        for t in range(TAPS):
+            zsrc_ref[g, 2 * t] = value[t, :8]
+            zsrc_ref[g, 2 * t + 1] = value[t, 8:]
+
+        def one(d, carry):
+            pz, device = z_partner(d)
+            send(zsrc_ref.at[g, pz], zr_ref.at[g, d - 1], ZSUM + g, device)
+            return carry
+
+        lax.fori_loop(1, n_z, one, 0)
+
+    def gather_z(g):
+        drain(zr_ref.at[g], rcv.at[ZSUM + g])
+        reduced = zsrc_ref[g, z] + jnp.sum(zr_ref[g], axis=0)
+        zred_ref[g] = reduced
+        zg_ref[g, z] = reduced
+
+        def one(d, carry):
+            send(zred_ref.at[g], zg_ref.at[g, z], ZALL + g, z_partner(d)[1])
+            return carry
+
+        lax.fori_loop(1, n_z, one, 0)
+
+    def gather_xy(g):
+        drain(zg_ref.at[g, 0 : n_z - 1], rcv.at[ZALL + g])
+        for t in range(TAPS):
+            ag_ref[g, core, mine, t] = jnp.concatenate([zg_ref[g, 2 * t], zg_ref[g, 2 * t + 1]], axis=0).astype(BF16)
+        own_piece = ag_ref.at[g, core, mine]
+        for dx in (0, 1, 3, 2):
+
+            def one(dy, carry):
+                send(own_piece, own_piece, XYALL + n_x * g + dx, xy_partner(dx * n_y + dy)[1])
+                return carry
+
+            lax.fori_loop(1 if dx == 0 else 0, n_y, one, 0)
+
+    last = []
+
+    def gather_core(g):
+        for dx in (0, 1, 3, 2):
+            count = n_y - 1 if dx == 0 else n_y
+            drain(ag_ref.at[g, 0, 0:count], rcv.at[XYALL + n_x * g + dx])
+            column = ag_ref.at[g, core, pl.ds(((x + n_x - dx) % n_x) * n_y, n_y)]
+            last.append(send(column, column, COREALL + n_x * g + dx, sibling))
+
     for t in range(3):
-        put(0, t, dot(actt_ref[...], gt_ref[2 - t : 2 - t + frames].reshape(frames * rows, chan)))
-    send_core(0)
+        put(t, dot(actt_ref[...], gt_ref[2 - t : 2 - t + frames].reshape(frames * rows, chan)))
 
     for f in range(frames):
         g_act = jnp.zeros((rows, chan), F32)
@@ -279,28 +356,30 @@
         ahead, behind = shifted(gs_ref, f)
         gs_ref[2, f] = ahead
         gs_ref[0, f] = behind
-    send_xy(0)
+    put_spatial(3)
+    send_core(0)
     head_copy.wait_recv()
     pair_rows = wg_ref.at[pl.ds(wide - core, CORES)]
     pair_copy = send(pair_rows, pair_rows, PAIR, pair)
 
-    for a in range(3):
-        for b in range(3):
-            window = gs_ref[b, :, 2 - a : 2 - a + side].reshape(frames * rows, chan)
-            put(1 + a, b, dot(xt_ref[...], window))
-        send_core(1 + a)
-        if a == 0:
-            pair_copy.wait_recv()
-            z_rows = wg_ref.at[pl.ds(z * (CORES * X_LO), CORES * X_LO)]
-
-            def send_head(d, carry):
-                send(z_rows, z_rows, ZHEAD, z_partner(d)[1])
-                return carry
-
-            lax.fori_loop(1, n_z, send_head, 0)
-        if a > 0:
-            send_xy(a)
-    send_xy(3)
+    for q in range(TAPS, 2 * TAPS):
+        put_spatial(q)
+    send_core(1)
+    send_xy(0)
+    pair_copy.wait_recv()
+    z_rows = wg_ref.at[pl.ds(z * (CORES * X_LO), CORES * X_LO)]
+
+    def send_head(d, carry):
+        send(z_rows, z_rows, ZHEAD, z_partner(d)[1])
+        return carry
+
+    lax.fori_loop(1, n_z, send_head, 0)
+    for q in range(2 * TAPS, 3 * TAPS):
+        put_spatial(q)
+    send_core(2)
+    send_xy(1)
+    send_xy(2)
+    sum_z(0)
 
     drain(wg_ref.at[0 : n_wide - CORES * X_LO], rcv.at[ZHEAD])
 
@@ -313,56 +392,23 @@
     zhat_all = all_clips(6, tiles)
     g_s_all = all_clips(10, shard // 128)
     gproj_ref[...] = lax.dot_general(pooled_all, g_z_all, over_clips, precision=HI, preferred_element_type=F32)
+    sum_z(1)
     g_phat = 16.0 * lax.dot_general(g_s_all, zhat_all, over_clips, precision=HI, preferred_element_type=F32)
     phat = ph_ref[...]
     p32 = pr_ref[...].astype(F32)
     pnorm = jnp.sqrt(jnp.sum(p32 * p32, axis=1, keepdims=True) + 1e-06)
     gprm_ref[...] = (g_phat - phat * jnp.sum(phat * g_phat, axis=1, keepdims=True)) / pnorm
 
-    for g in range(4):
-        drain(xyr_ref.at[g], rcv.at[XY + g])
-        value = cs_ref[g, mine].astype(F32)
-        for d in range(n_xy - 1):
-            value = value + xyr_ref[g, d].astype(F32)
-        for t in range(3):
-            zsrc_ref[6 * g + 2 * t] = value[t, :8]
-            zsrc_ref[6 * g + 2 * t + 1] = value[t, 8:]
-    chunk = 24 // n_z
-
-    def send_zsum(d, carry):
-        pz, device = z_partner(d)
-        send(zsrc_ref.at[pl.ds(pz * chunk, chunk)], zr_ref.at[d - 1], ZSUM, device)
-        return carry
-
-    lax.fori_loop(1, n_z, send_zsum, 0)
-    drain(zr_ref, rcv.at[ZSUM])
-    own = pl.ds(z * chunk, chunk)
-    reduced = zsrc_ref[own] + jnp.sum(zr_ref[...], axis=0)
-    zred_ref[...] = reduced
-    zg_ref[own] = reduced
-
-    def send_zall(d, carry):
-        send(zred_ref, zg_ref.at[own], ZALL, z_partner(d)[1])
-        return carry
-
-    lax.fori_loop(1, n_z, send_zall, 0)
-    drain(zg_ref.at[0 : 24 - chunk], rcv.at[ZALL])
-    for q in range(12):
-        ag_ref[core, mine, q] = jnp.concatenate([zg_ref[2 * q], zg_ref[2 * q + 1]], axis=0).astype(BF16)
-    own_piece = ag_ref.at[core, mine]
-    for dx in (0, 1, 3, 2):
-
-        def send_piece(dy, carry):
-            send(own_piece, own_piece, XYALL + dx, xy_partner(dx * n_y + dy)[1])
-            return carry
-
-        lax.fori_loop(1 if dx == 0 else 0, n_y, send_piece, 0)
-    last = []
-    for dx in (0, 1, 3, 2):
-        count = n_y - 1 if dx == 0 else n_y
-        drain(ag_ref.at[0, 0:count], rcv.at[XYALL + dx])
-        column = ag_ref.at[core, pl.ds(((x + n_x - dx) % n_x) * n_y, n_y)]
-        last.append(send(column, column, COREALL + dx, sibling))
+    gather_z(0)
+    sum_z(2)
+    gather_z(1)
+    gather_xy(0)
+    gather_z(2)
+    gather_xy(1)
+    gather_core(0)
+    gather_xy(2)
+    gather_core(1)
+    gather_core(2)
     for copy in last:
         copy.wait_recv()
 
@@ -371,12 +417,12 @@
     drain(pool_ref.at[0 : n_tm - 1], snd.at[POOL])
     drain(ab_ref.at[0 : n_tm - 1], snd.at[AB])
     drain(wg_ref.at[0 : n_wide - CORES * X_LO], snd.at[ZHEAD])
-    for g in range(4):
+    for g in range(GROUPS):
         drain(xyr_ref.at[g], snd.at[XY + g])
-    drain(zr_ref, snd.at[ZSUM])
-    drain(zg_ref.at[0 : 24 - chunk], snd.at[ZALL])
-    for dx in range(n_x):
-        drain(ag_ref.at[0, 0 : n_y - 1 if dx == 0 else n_y], snd.at[XYALL + dx])
+        drain(zr_ref.at[g], snd.at[ZSUM + g])
+        drain(zg_ref.at[g, 0 : n_z - 1], snd.at[ZALL + g])
+        for dx in range(n_x):
+            drain(ag_ref.at[g, 0, 0 : n_y - 1 if dx == 0 else n_y], snd.at[XYALL + n_x * g + dx])
 
 
 def lay_kernel(ag_ref, gproj_ref, gprm_ref, gs_out, gt_out, gproj_out, gprm_out, buf_ref, sems):
@@ -386,14 +432,14 @@
     ]
     for copy in copies:
         copy.start()
-    cores, pieces, taps = ag_ref.shape[:3]
+    groups, cores, pieces, taps = ag_ref.shape[:4]
     half = buf_ref.shape[1] // cores
-    for q in range(taps):
+    for q in range(groups * taps):
         for c in range(cores):
             for p in range(pieces):
                 i, j = p // 2, p % 2
                 r = half * c + 16 * i
-                buf_ref[q, r : r + 16, 128 * j : 128 * (j + 1)] = ag_ref[c, p, q].astype(F32)
+                buf_ref[q, r : r + 16, 128 * j : 128 * (j + 1)] = ag_ref[q // taps, c, p, q % taps].astype(F32)
         target = gt_out.at[q] if q < 3 else gs_out.at[q - 3]
         copies.append(pltpu.make_async_copy(buf_ref.at[q], target, sems.at[q]))
         copies[-1].start()
@@ -410,16 +456,16 @@
     n_xy = X_HI * X_LO * (n_tm // X_HI)
     sizes = (n_wide, n_tm, frames, side, chan, embed, shard)
     vmem = pl.BlockSpec(memory_space=pltpu.VMEM)
-    smem = pl.BlockSpec(memory_space=pltpu.SMEM)
+    hbm = pl.BlockSpec(memory_space=pltpu.HBM)
     half = chan // 2
     gathered, grad_proj, grad_prompts = pl.pallas_call(
         functools.partial(step_kernel, sizes),
         out_shape=(
-            jax.ShapeDtypeStruct((CORES, n_xy, 12, 16, 128), BF16),
+            jax.ShapeDtypeStruct((GROUPS, CORES, n_xy, TAPS, 16, 128), BF16),
             jax.ShapeDtypeStruct((chan, embed), F32),
             jax.ShapeDtypeStruct((shard, embed), F32),
         ),
-        in_specs=[vmem] * 5 + [smem],
+        in_specs=[vmem] + [hbm] * 5,
         out_specs=(vmem, vmem, vmem),
         scratch_shapes=[
             pltpu.VMEM((3, frames, side + 2, LINE, chan), BF16),
@@ -437,16 +483,22 @@
             pltpu.VMEM((n_tm, 8, chan), F32),
             pltpu.VMEM((n_tm, 2, 8, 128), F32),
             pltpu.VMEM((n_wide, 16, 128), F32),
-            pltpu.VMEM((4, 2, 3, half, chan), F32),
-            pltpu.VMEM((4, 3, half, chan), F32),
-            pltpu.VMEM((4, n_xy, 3, 16, 128), BF16),
-            pltpu.VMEM((4, n_xy - 1, 3, 16, 128), BF16),
-            pltpu.VMEM((24, 8, 128), F32),
-            pltpu.VMEM((n_z - 1, 24 // n_z, 8, 128), F32),
-            pltpu.VMEM((24 // n_z, 8, 128), F32),
-            pltpu.VMEM((24, 8, 128), F32),
+            pltpu.VMEM((GROUPS, 2, TAPS, half, chan), F32),
+            pltpu.VMEM((GROUPS, TAPS, half, chan), F32),
+            pltpu.VMEM((GROUPS, n_xy, TAPS, 16, 128), BF16),
+            pltpu.VMEM((GROUPS, n_xy - 1, TAPS, 16, 128), BF16),
+            pltpu.VMEM((GROUPS, n_z, 8, 128), F32),
+            pltpu.VMEM((GROUPS, n_z - 1, 8, 128), F32),
+            pltpu.VMEM((GROUPS, 8, 128), F32),
+            pltpu.VMEM((GROUPS, n_z, 8, 128), F32),
+            pltpu.VMEM((9, chan, chan), BF16),
+            pltpu.VMEM((3, chan, chan), BF16),
+            pltpu.VMEM((chan, embed), BF16),
+            pltpu.VMEM((shard, embed), BF16),
+            pltpu.VMEM(positives.shape, jnp.int32),
             pltpu.SemaphoreType.DMA((SEMS,)),
             pltpu.SemaphoreType.DMA((SEMS,)),
+            pltpu.SemaphoreType.DMA((5,)),
         ],
         compiler_params=pltpu.CompilerParams(
             collective_id=0, has_side_effects=True, vmem_limit_bytes=48 * 1024 * 1024
@@ -465,6 +517,7 @@
         in_specs=[vmem] * 3,
         out_specs=(anywhere,) * 4,
         scratch_shapes=[pltpu.VMEM((12, chan, chan), F32), pltpu.SemaphoreType.DMA((14,))],
+        compiler_params=pltpu.CompilerParams(vmem_limit_bytes=8 * 1024 * 1024),
         name="lay_out",
     )(gathered, grad_proj, grad_prompts)
     return grad_s.reshape(3, 3, chan, chan), grad_t, grad_p, grad_m

time: 81.7 us -> 72.2 us (0.88)
  Pallas kernels: 71.9 us -> 65.3 us
  local copies, waits for them, and re-layouts: 8.87 us -> 5.97 us
    pallas_call x1, Pallas kernels: 67.8 us -> 63 us  [body(): pl.pallas_call(functools.partial(step_kernel, sizes), out_shape=(jax.Shap...]
    unnamed x17 -> x11, local copies, waits for them, and re-layouts: 8.87 us -> 5.97 us
    pallas_call x1, Pallas kernels: 4.14 us -> 2.28 us  [body(): pl.pallas_call(lay_kernel, out_shape=(jax.ShapeDtypeStruct((9, chan, chan...]
where the time goes in v2:
time: 72.2 us; the launch traced here: 71.9 us
  Pallas kernels  65.3 us (90%)
  local copies, waits for them, and re-layouts  5.97 us (8%)
    pallas_call x1, Pallas kernels, body(): pl.pallas_call(functools.partial(step_kernel, sizes), out_shape=(jax.Shap...  63 us
    unnamed x11, local copies, waits for them, and re-layouts  5.97 us
    pallas_call x1, Pallas kernels, body(): pl.pallas_call(lay_kernel, out_shape=(jax.ShapeDtypeStruct((9, chan, chan...  2.28 us

profile of v2, /device:TPU:1, one launch (start us, length us, event | category | flops | bytes accessed | tf_op | source)
XLA Modules:
  0.0 71.9 jit_solution(5650630141849572218)
XLA Ops:
  0.6 1.1 %copy.10.x_ref = bf16[1,4,14,14,256]{4,3,2,1,0:T(8,128)(2,1)S(1)} copy(bf16[1,4,14,14,256]{4,1,3,2,0:T(4,128)(2,1)} %param.6) | data formatting | bytes 802816 | tf_op args[0]
  1.7 0.0 copy-start
  1.7 1.3 %copy-done = bf16[3,3,256,256]{3,2,1,0:T(8,128)(2,1)S(1)} copy-done((bf16[3,3,256,256]{3,2,1,0:T(8,128)(2,1)S(1)}, bf16[3,3,256,256]{3,2,1,0:T(8,128)(2,1)}, u32[]{:S(2)}) %copy-start) | copy-done | bytes 1179672
  3.0 0.0 copy-start.1
  3.0 1.0 %copy-done.1 = bf16[512,512]{1,0:T(8,128)(2,1)S(1)} copy-done((bf16[512,512]{1,0:T(8,128)(2,1)S(1)}, bf16[512,512]{1,0:T(8,128)(2,1)}, u32[]{:S(2)}) %copy-start.1) | copy-done | bytes 524312
  4.0 0.0 copy-start.2
  4.0 1.0 %copy-done.2 = bf16[3,256,256]{2,1,0:T(8,128)(2,1)S(1)} copy-done((bf16[3,256,256]{2,1,0:T(8,128)(2,1)S(1)}, bf16[3,256,256]{2,1,0:T(8,128)(2,1)}, u32[]{:S(2)}) %copy-start.2) | copy-done | bytes 393240
  5.0 0.0 copy-start.3
  5.0 0.9 %copy-done.3 = bf16[256,512]{1,0:T(8,128)(2,1)S(1)} copy-done((bf16[256,512]{1,0:T(8,128)(2,1)S(1)}, bf16[256,512]{1,0:T(8,128)(2,1)}, u32[]{:S(2)}) %copy-start.3) | copy-done | bytes 262168
  6.0 0.0 copy-start.4
  6.0 0.7 copy-done.4
  6.6 63.0 %step.1 = (bf16[3,2,16,4,16,128]{5,4,3,2,1,0:T(8,128)(2,1)S(1)}, f32[256,512]{1,0:T(8,128)S(1)}, f32[512,512]{1,0:T(8,128)S(1)}) custom-call(bf16[1,4,14,14,256]{4,3,2,1,0:T(8,128)(2,1)S(1)} %copy.10.x_ref, bf16[9,256,256]{2,1,0:T(8,128)(2,1)S(1)} %bitcast.2, bf16[3,256,256]{2,1,0:T(8,128)(2,1)S(1)} %copy-done.2, bf16[256,512]{1,0:T(8,128)(2,1)S(1)} %copy-done.3, ...), custom_call_target="tpu_custom_call" | custom-call | tf_op jit(solution)/shard_map/step/pallas_call | solution.py:461
  69.6 2.3 %lay_out.1 = (f32[9,256,256]{2,1,0:T(8,128)}, f32[3,256,256]{2,1,0:T(8,128)}, f32[256,512]{1,0:T(8,128)}, f32[512,512]{1,0:T(8,128)}) custom-call(bf16[3,2,16,4,16,128]{5,4,3,2,1,0:T(8,128)(2,1)S(1)} %get-tuple-element.11.ag_ref, f32[256,512]{1,0:T(8,128)S(1)} %get-tuple-element.12.gproj_ref, f32[512,512]{1,0:T(8,128)S(1)} %get-tuple-element.13.gprm_ref), custom_call_target="tpu_custom_call" | custom-call | tf_op jit(solution)/shard_map/lay_out/pallas_call | solution.py:509
Async XLA Ops:
  1.7 1.3 %copy-start = (bf16[3,3,256,256]{3,2,1,0:T(8,128)(2,1)S(1)}, bf16[3,3,256,256]{3,2,1,0:T(8,128)(2,1)}, u32[]{:S(2)}) copy-start(bf16[3,3,256,256]{3,2,1,0:T(8,128)(2,1)} %param.7) | copy-start | bytes 3538948
  3.0 1.0 %copy-start.1 = (bf16[512,512]{1,0:T(8,128)(2,1)S(1)}, bf16[512,512]{1,0:T(8,128)(2,1)}, u32[]{:S(2)}) copy-start(bf16[512,512]{1,0:T(8,128)(2,1)} %pr_hbm.1) | copy-start | bytes 1572868
  4.0 1.0 %copy-start.2 = (bf16[3,256,256]{2,1,0:T(8,128)(2,1)S(1)}, bf16[3,256,256]{2,1,0:T(8,128)(2,1)}, u32[]{:S(2)}) copy-start(bf16[3,256,256]{2,1,0:T(8,128)(2,1)} %wt_hbm.1) | copy-start | bytes 1179652
  5.0 0.9 %copy-start.3 = (bf16[256,512]{1,0:T(8,128)(2,1)S(1)}, bf16[256,512]{1,0:T(8,128)(2,1)}, u32[]{:S(2)}) copy-start(bf16[256,512]{1,0:T(8,128)(2,1)} %wp_hbm.1) | copy-start | bytes 786436
  6.0 0.7 copy-start.4

commit v3 on v2

--- a/solution.py
+++ b/solution.py
@@ -51,12 +51,12 @@
 
 def step_kernel(
     sizes,
-    x_ref, ws_hbm, wt_hbm, wp_hbm, pr_hbm, pos_hbm,
-    ag_ref, gproj_ref, gprm_ref,
+    x_hbm, ws_hbm, wt_hbm, wp_hbm, pr_hbm, pos_hbm,
+    ag_hbm, gproj_hbm, gprm_hbm,
     xs_ref, pre_ref, act_ref, dt_ref, dsend_ref, dhalo_ref, gt_ref, gs_ref, xt_ref, actt_ref, wtt_ref,
     ph_ref, pool_ref, ab_ref, wg_ref, gbuf_ref, rbuf_ref, cs_ref, xyr_ref, zsrc_ref, zr_ref, zred_ref, zg_ref,
-    ws_ref, wt_ref, wp_ref, pr_ref, pos_ref,
-    snd, rcv, loc,
+    ws_ref, wt_ref, wp_ref, pr_ref, pos_ref, x_ref, ag_ref, gproj_ref, gprm_ref,
+    snd, rcv, loc, out,
 ):
     n_wide, n_tm, frames, side, chan, embed, shard = sizes
     rows = side * LINE
@@ -99,12 +99,15 @@
     loads = [
         pltpu.make_async_copy(src, dst, loc.at[i])
         for i, (src, dst) in enumerate(
-            [(ws_hbm, ws_ref), (pr_hbm, pr_ref), (wt_hbm, wt_ref), (wp_hbm, wp_ref), (pos_hbm, pos_ref)]
+            [
+                (x_hbm, x_ref), (ws_hbm, ws_ref), (pr_hbm, pr_ref),
+                (wt_hbm, wt_ref), (wp_hbm, wp_ref), (pos_hbm, pos_ref),
+            ]
         )
     ]
     for load in loads:
         load.start()
-    load_ws, load_pr, load_wt, load_wp, load_pos = loads
+    load_x, load_ws, load_pr, load_wt, load_wp, load_pos = loads
 
     barrier = pltpu.get_barrier_semaphore()
 
@@ -150,6 +153,7 @@
     left = (wide, (tm + n_tm - 1) % n_tm)
     right = (wide, (tm + 1) % n_tm)
 
+    load_x.wait()
     window(0)
     window(frames - 1)
     load_ws.wait()
@@ -398,6 +402,19 @@
     p32 = pr_ref[...].astype(F32)
     pnorm = jnp.sqrt(jnp.sum(p32 * p32, axis=1, keepdims=True) + 1e-06)
     gprm_ref[...] = (g_phat - phat * jnp.sum(phat * g_phat, axis=1, keepdims=True)) / pnorm
+    results = [
+        pltpu.make_async_copy(gproj_ref, gproj_hbm, out.at[GROUPS]),
+        pltpu.make_async_copy(gprm_ref, gprm_hbm, out.at[GROUPS + 1]),
+    ]
+    for result in results:
+        result.start()
+
+    def put_out(g):
+        for copy in last[n_x * g : n_x * (g + 1)]:
+            copy.wait_recv()
+        result = pltpu.make_async_copy(ag_ref.at[g], ag_hbm.at[g], out.at[g])
+        result.start()
+        results.append(result)
 
     gather_z(0)
     sum_z(2)
@@ -408,9 +425,10 @@
     gather_core(0)
     gather_xy(2)
     gather_core(1)
+    put_out(0)
     gather_core(2)
-    for copy in last:
-        copy.wait_recv()
+    put_out(1)
+    put_out(2)
 
     for copy in [to_left, to_right, d_left, d_right, head_copy, pair_copy] + core_copies + last:
         copy.wait_send()
@@ -423,18 +441,25 @@
         drain(zg_ref.at[g, 0 : n_z - 1], snd.at[ZALL + g])
         for dx in range(n_x):
             drain(ag_ref.at[g, 0, 0 : n_y - 1 if dx == 0 else n_y], snd.at[XYALL + n_x * g + dx])
-
-
-def lay_kernel(ag_ref, gproj_ref, gprm_ref, gs_out, gt_out, gproj_out, gprm_out, buf_ref, sems):
-    copies = [
-        pltpu.make_async_copy(gprm_ref, gprm_out, sems.at[12]),
-        pltpu.make_async_copy(gproj_ref, gproj_out, sems.at[13]),
-    ]
-    for copy in copies:
-        copy.start()
+    for result in results:
+        result.wait()
+
+
+def lay_kernel(
+    ag_hbm, gproj_hbm, gprm_hbm, gs_out, gt_out, gproj_out, gprm_out,
+    ag_ref, gproj_ref, gprm_ref, buf_ref, load_sems, sems,
+):
     groups, cores, pieces, taps = ag_ref.shape[:4]
+    loads = [pltpu.make_async_copy(ag_hbm.at[g], ag_ref.at[g], load_sems.at[g]) for g in range(groups)]
+    loads.append(pltpu.make_async_copy(gprm_hbm, gprm_ref, load_sems.at[groups]))
+    loads.append(pltpu.make_async_copy(gproj_hbm, gproj_ref, load_sems.at[groups + 1]))
+    for load in loads:
+        load.start()
+    copies = []
     half = buf_ref.shape[1] // cores
     for q in range(groups * taps):
+        if q % taps == 0:
+            loads[q // taps].wait()
         for c in range(cores):
             for p in range(pieces):
                 i, j = p // 2, p % 2
@@ -443,6 +468,12 @@
         target = gt_out.at[q] if q < 3 else gs_out.at[q - 3]
         copies.append(pltpu.make_async_copy(buf_ref.at[q], target, sems.at[q]))
         copies[-1].start()
+    loads[groups].wait()
+    copies.append(pltpu.make_async_copy(gprm_ref, gprm_out, sems.at[12]))
+    copies[-1].start()
+    loads[groups + 1].wait()
+    copies.append(pltpu.make_async_copy(gproj_ref, gproj_out, sems.at[13]))
+    copies[-1].start()
     for copy in copies:
         copy.wait()
 
@@ -455,7 +486,6 @@
     n_z = n_wide // (X_LO * CORES)
     n_xy = X_HI * X_LO * (n_tm // X_HI)
     sizes = (n_wide, n_tm, frames, side, chan, embed, shard)
-    vmem = pl.BlockSpec(memory_space=pltpu.VMEM)
     hbm = pl.BlockSpec(memory_space=pltpu.HBM)
     half = chan // 2
     gathered, grad_proj, grad_prompts = pl.pallas_call(
@@ -465,8 +495,8 @@
             jax.ShapeDtypeStruct((chan, embed), F32),
             jax.ShapeDtypeStruct((shard, embed), F32),
         ),
-        in_specs=[vmem] + [hbm] * 5,
-        out_specs=(vmem, vmem, vmem),
+        in_specs=[hbm] * 6,
+        out_specs=(hbm,) * 3,
         scratch_shapes=[
             pltpu.VMEM((3, frames, side + 2, LINE, chan), BF16),
             pltpu.VMEM((frames, rows, chan), F32),
@@ -496,16 +526,20 @@
             pltpu.VMEM((chan, embed), BF16),
             pltpu.VMEM((shard, embed), BF16),
             pltpu.VMEM(positives.shape, jnp.int32),
+            pltpu.VMEM(clips_in.shape, BF16),
+            pltpu.VMEM((GROUPS, CORES, n_xy, TAPS, 16, 128), BF16),
+            pltpu.VMEM((chan, embed), F32),
+            pltpu.VMEM((shard, embed), F32),
             pltpu.SemaphoreType.DMA((SEMS,)),
             pltpu.SemaphoreType.DMA((SEMS,)),
-            pltpu.SemaphoreType.DMA((5,)),
+            pltpu.SemaphoreType.DMA((6,)),
+            pltpu.SemaphoreType.DMA((GROUPS + 2,)),
         ],
         compiler_params=pltpu.CompilerParams(
-            collective_id=0, has_side_effects=True, vmem_limit_bytes=48 * 1024 * 1024
+            collective_id=0, has_side_effects=True, vmem_limit_bytes=66_500_000
         ),
         name="step",
     )(clips_in, w_spatial.reshape(9, chan, chan), w_temporal, w_proj, prompts, positives)
-    anywhere = pl.BlockSpec(memory_space=pl.ANY)
     grad_s, grad_t, grad_p, grad_m = pl.pallas_call(
         lay_kernel,
         out_shape=(
@@ -514,10 +548,17 @@
             jax.ShapeDtypeStruct((chan, embed), F32),
             jax.ShapeDtypeStruct((shard, embed), F32),
         ),
-        in_specs=[vmem] * 3,
-        out_specs=(anywhere,) * 4,
-        scratch_shapes=[pltpu.VMEM((12, chan, chan), F32), pltpu.SemaphoreType.DMA((14,))],
-        compiler_params=pltpu.CompilerParams(vmem_limit_bytes=8 * 1024 * 1024),
+        in_specs=[hbm] * 3,
+        out_specs=(hbm,) * 4,
+        scratch_shapes=[
+            pltpu.VMEM((GROUPS, CORES, n_xy, TAPS, 16, 128), BF16),
+            pltpu.VMEM((chan, embed), F32),
+            pltpu.VMEM((shard, embed), F32),
+            pltpu.VMEM((12, chan, chan), F32),
+            pltpu.SemaphoreType.DMA((GROUPS + 2,)),
+            pltpu.SemaphoreType.DMA((14,)),
+        ],
+        compiler_params=pltpu.CompilerParams(vmem_limit_bytes=66_500_000),
         name="lay_out",
     )(gathered, grad_proj, grad_prompts)
     return grad_s.reshape(3, 3, chan, chan), grad_t, grad_p, grad_m

time: 72.2 us -> 68.9 us (0.954)
  local copies, waits for them, and re-layouts: 5.97 us -> 1.83 us
  Pallas kernels: 65.3 us -> 66.3 us
    unnamed x11 -> x1, local copies, waits for them, and re-layouts: 5.97 us -> 1.83 us
    pallas_call x1, Pallas kernels: 2.28 us -> 3.4 us  [body(): pl.pallas_call(lay_kernel, out_shape=(jax.ShapeDtypeStruct((9, chan, chan...]
where the time goes in v3:
time: 68.9 us; the launch traced here: 68.8 us
  Pallas kernels  66.3 us (96%)
  local copies, waits for them, and re-layouts  1.83 us (3%)
    pallas_call x1, Pallas kernels, body(): pl.pallas_call(functools.partial(step_kernel, sizes), out_shape=(jax.Shap...  62.9 us
    pallas_call x1, Pallas kernels, body(): pl.pallas_call(lay_kernel, out_shape=(jax.ShapeDtypeStruct((9, chan, chan...  3.4 us
    unnamed x1, local copies, waits for them, and re-layouts  1.83 us

profile of v3, /device:TPU:1, one launch (start us, length us, event | category | flops | bytes accessed | tf_op | source)
XLA Modules:
  0.0 68.8 jit_solution(2200573544017040089)
XLA Ops:
  0.6 1.8 %copy.10.x_hbm = bf16[1,4,14,14,256]{4,3,2,1,0:T(8,128)(2,1)} copy(bf16[1,4,14,14,256]{4,1,3,2,0:T(4,128)(2,1)} %param.6) | data formatting | bytes 802816 | tf_op args[0]
  2.5 62.9 %step.1 = (bf16[3,2,16,4,16,128]{5,4,3,2,1,0:T(8,128)(2,1)}, f32[256,512]{1,0:T(8,128)}, f32[512,512]{1,0:T(8,128)}) custom-call(bf16[1,4,14,14,256]{4,3,2,1,0:T(8,128)(2,1)} %copy.10.x_hbm, bf16[9,256,256]{2,1,0:T(8,128)(2,1)} %bitcast.2, bf16[3,256,256]{2,1,0:T(8,128)(2,1)} %wt_hbm.1, bf16[256,512]{1,0:T(8,128)(2,1)} %wp_hbm.1, bf16[512,512]{1,0:T(8,128)(2,1)} %pr_hbm.1, ...), custom_call_target="tpu_custom_call" | custom-call | tf_op jit(solution)/shard_map/step/pallas_call | solution.py:491
  65.4 3.4 %lay_out.1 = (f32[9,256,256]{2,1,0:T(8,128)}, f32[3,256,256]{2,1,0:T(8,128)}, f32[256,512]{1,0:T(8,128)}, f32[512,512]{1,0:T(8,128)}) custom-call(bf16[3,2,16,4,16,128]{5,4,3,2,1,0:T(8,128)(2,1)} %get-tuple-element.11.ag_hbm, f32[256,512]{1,0:T(8,128)} %get-tuple-element.12.gproj_hbm, f32[512,512]{1,0:T(8,128)} %get-tuple-element.13.gprm_hbm), custom_call_target="tpu_custom_call" | custom-call | tf_op jit(solution)/shard_map/lay_out/pallas_call | solution.py:543

commit v4 on v3

--- a/solution.py
+++ b/solution.py
@@ -165,10 +165,6 @@
     for f in range(1, frames - 1):
         window(f)
         conv(f)
-    load_pr.wait()
-    p32 = pr_ref[...].astype(F32)
-    pnorm = jnp.sqrt(jnp.sum(p32 * p32, axis=1, keepdims=True) + 1e-06)
-    ph_ref[...] = p32 / pnorm
 
     pooled8 = jnp.zeros((8, chan), F32)
     for f in range(frames):
@@ -176,9 +172,11 @@
             xs_ref[1, f, 1 : side + 1].reshape(rows // 8, 8, chan).astype(F32), axis=0
         )
     load_wt.wait()
-    to_right.wait_recv()
-    to_left.wait_recv()
     for f in list(range(1, frames - 1)) + [0, frames - 1]:
+        if f == 0:
+            to_right.wait_recv()
+        if f == frames - 1:
+            to_left.wait_recv()
         below = dot(act_ref[f], wt_ref[0])
         above = dot(act_ref[f + 2], wt_ref[2])
         if f == 0:
@@ -205,14 +203,16 @@
     d_left = send(dsend_ref.at[0], dhalo_ref.at[1], DHALO + 1, left)
     d_right = send(dsend_ref.at[1], dhalo_ref.at[0], DHALO, right)
     for f in range(frames):
-        pre_ref[f] = dsilu(pre_ref[f])
-        xt_ref[:, f * rows : (f + 1) * rows] = xs_ref[1, f, 1 : side + 1].reshape(rows, chan).T
         actt_ref[:, f * rows : (f + 1) * rows] = act_ref[f + 1].T
         for b in range(3):
             gs_ref[b, f, 0] = jnp.zeros((LINE, chan), BF16)
             gs_ref[b, f, side + 1] = jnp.zeros((LINE, chan), BF16)
     for t in range(3):
         wtt_ref[t] = wt_ref[t].T
+    load_pr.wait()
+    p32 = pr_ref[...].astype(F32)
+    pnorm = jnp.sqrt(jnp.sum(p32 * p32, axis=1, keepdims=True) + 1e-06)
+    ph_ref[...] = p32 / pnorm
     load_wp.wait()
     load_pos.wait()
     wp = wp_ref[...].astype(F32)
@@ -242,6 +242,9 @@
         return carry
 
     lax.fori_loop(1, n_tm, send_ab, 0)
+    for f in range(frames):
+        pre_ref[f] = dsilu(pre_ref[f])
+        xt_ref[:, f * rows : (f + 1) * rows] = xs_ref[1, f, 1 : side + 1].reshape(rows, chan).T
     drain(ab_ref.at[0 : n_tm - 1], rcv.at[AB])
     summed = jnp.sum(ab_ref[...], axis=0)
     sum_a = jnp.concatenate([summed[0, k : k + 1] for k in range(tiles)], axis=1)

time: 68.9 us -> 69 us (level)
  no operation moved by 1% of the time
where the time goes in v4:
time: 69 us; the launch traced here: 68.8 us
  Pallas kernels  66.3 us (96%)
  local copies, waits for them, and re-layouts  1.83 us (3%)
    pallas_call x1, Pallas kernels, body(): pl.pallas_call(functools.partial(step_kernel, sizes), out_shape=(jax.Shap...  62.9 us
    pallas_call x1, Pallas kernels, body(): pl.pallas_call(lay_kernel, out_shape=(jax.ShapeDtypeStruct((9, chan, chan...  3.4 us
    unnamed x1, local copies, waits for them, and re-layouts  1.83 us

profile of v4, /device:TPU:1, one launch (start us, length us, event | category | flops | bytes accessed | tf_op | source)
XLA Modules:
  0.0 68.8 jit_solution(1855078716503123243)
XLA Ops:
  0.6 1.8 %copy.10.x_hbm = bf16[1,4,14,14,256]{4,3,2,1,0:T(8,128)(2,1)} copy(bf16[1,4,14,14,256]{4,1,3,2,0:T(4,128)(2,1)} %param.6) | data formatting | bytes 802816 | tf_op args[0]
  2.5 62.9 %step.1 = (bf16[3,2,16,4,16,128]{5,4,3,2,1,0:T(8,128)(2,1)}, f32[256,512]{1,0:T(8,128)}, f32[512,512]{1,0:T(8,128)}) custom-call(bf16[1,4,14,14,256]{4,3,2,1,0:T(8,128)(2,1)} %copy.10.x_hbm, bf16[9,256,256]{2,1,0:T(8,128)(2,1)} %bitcast.2, bf16[3,256,256]{2,1,0:T(8,128)(2,1)} %wt_hbm.1, bf16[256,512]{1,0:T(8,128)(2,1)} %wp_hbm.1, bf16[512,512]{1,0:T(8,128)(2,1)} %pr_hbm.1, ...), custom_call_target="tpu_custom_call" | custom-call | tf_op jit(solution)/shard_map/step/pallas_call | solution.py:494
  65.4 3.4 %lay_out.1 = (f32[9,256,256]{2,1,0:T(8,128)}, f32[3,256,256]{2,1,0:T(8,128)}, f32[256,512]{1,0:T(8,128)}, f32[512,512]{1,0:T(8,128)}) custom-call(bf16[3,2,16,4,16,128]{5,4,3,2,1,0:T(8,128)(2,1)} %get-tuple-element.11.ag_hbm, f32[256,512]{1,0:T(8,128)} %get-tuple-element.12.gproj_hbm, f32[512,512]{1,0:T(8,128)} %get-tuple-element.13.gprm_hbm), custom_call_target="tpu_custom_call" | custom-call | tf_op jit(solution)/shard_map/lay_out/pallas_call | solution.py:546

commit v5 on v4

--- a/solution.py
+++ b/solution.py
@@ -143,10 +143,8 @@
         xs_ref[2, f] = behind
 
     def conv(f):
-        total = jnp.zeros((rows, chan), F32)
-        for a in range(3):
-            for b in range(3):
-                total = total + dot(xs_ref[b, f, a : a + side].reshape(rows, chan), ws_ref[3 * a + b])
+        windows = [xs_ref[b, f, a : a + side].reshape(rows, chan) for a in range(3) for b in range(3)]
+        total = dot(jnp.concatenate(windows, axis=1), ws_ref[...].reshape(9 * chan, chan))
         pre_ref[f] = total
         act_ref[f + 1] = jnp.where(inside, total * sigmoid(total), 0.0).astype(BF16)
 
@@ -335,7 +333,7 @@
         for t in range(TAPS):
             ag_ref[g, core, mine, t] = jnp.concatenate([zg_ref[g, 2 * t], zg_ref[g, 2 * t + 1]], axis=0).astype(BF16)
         own_piece = ag_ref.at[g, core, mine]
-        for dx in (0, 1, 3, 2):
+        for dx in (2, 1, 3, 0):
 
             def one(dy, carry):
                 send(own_piece, own_piece, XYALL + n_x * g + dx, xy_partner(dx * n_y + dy)[1])
@@ -356,9 +354,8 @@
         put(t, dot(actt_ref[...], gt_ref[2 - t : 2 - t + frames].reshape(frames * rows, chan)))
 
     for f in range(frames):
-        g_act = jnp.zeros((rows, chan), F32)
-        for t in range(3):
-            g_act = g_act + dot(gt_ref[f + 2 - t], wtt_ref[t])
+        near = jnp.concatenate([gt_ref[f + 2 - t] for t in range(3)], axis=1)
+        g_act = dot(near, wtt_ref[...].reshape(3 * chan, chan))
         gs_ref[1, f, 1 : side + 1] = (g_act * pre_ref[f]).astype(BF16).reshape(side, LINE, chan)
         ahead, behind = shifted(gs_ref, f)
         gs_ref[2, f] = ahead

time: 69 us -> 68.3 us (0.990)
  no operation moved by 1% of the time
where the time goes in v5:
time: 68.3 us; the launch traced here: 68.2 us
  Pallas kernels  65.7 us (96%)
  local copies, waits for them, and re-layouts  1.83 us (3%)
    pallas_call x1, Pallas kernels, body(): pl.pallas_call(functools.partial(step_kernel, sizes), out_shape=(jax.Shap...  62.3 us
    pallas_call x1, Pallas kernels, body(): pl.pallas_call(lay_kernel, out_shape=(jax.ShapeDtypeStruct((9, chan, chan...  3.4 us
    unnamed x1, local copies, waits for them, and re-layouts  1.83 us

profile of v5, /device:TPU:1, one launch (start us, length us, event | category | flops | bytes accessed | tf_op | source)
XLA Modules:
  0.0 68.2 jit_solution(13339860683000812519)
XLA Ops:
  0.6 1.8 %copy.10.x_hbm = bf16[1,4,14,14,256]{4,3,2,1,0:T(8,128)(2,1)} copy(bf16[1,4,14,14,256]{4,1,3,2,0:T(4,128)(2,1)} %param.6) | data formatting | bytes 802816 | tf_op args[0]
  2.5 62.3 %step.1 = (bf16[3,2,16,4,16,128]{5,4,3,2,1,0:T(8,128)(2,1)}, f32[256,512]{1,0:T(8,128)}, f32[512,512]{1,0:T(8,128)}) custom-call(bf16[1,4,14,14,256]{4,3,2,1,0:T(8,128)(2,1)} %copy.10.x_hbm, bf16[9,256,256]{2,1,0:T(8,128)(2,1)} %bitcast.2, bf16[3,256,256]{2,1,0:T(8,128)(2,1)} %wt_hbm.1, bf16[256,512]{1,0:T(8,128)(2,1)} %wp_hbm.1, bf16[512,512]{1,0:T(8,128)(2,1)} %pr_hbm.1, ...), custom_call_target="tpu_custom_call" | custom-call | tf_op jit(solution)/shard_map/step/pallas_call | solution.py:491
  64.8 3.4 %lay_out.1 = (f32[9,256,256]{2,1,0:T(8,128)}, f32[3,256,256]{2,1,0:T(8,128)}, f32[256,512]{1,0:T(8,128)}, f32[512,512]{1,0:T(8,128)}) custom-call(bf16[3,2,16,4,16,128]{5,4,3,2,1,0:T(8,128)(2,1)} %get-tuple-element.11.ag_hbm, f32[256,512]{1,0:T(8,128)} %get-tuple-element.12.gproj_hbm, f32[512,512]{1,0:T(8,128)} %get-tuple-element.13.gprm_hbm), custom_call_target="tpu_custom_call" | custom-call | tf_op jit(solution)/shard_map/lay_out/pallas_call | solution.py:543
